TPU v7x, 256 devices: a whole 4x4x8 slice. The times are simulated.
256 devices in a mesh: trow: 4 (over y), tcol: 4 (over x), pix: 16 (over z, core).
Axes of the slice: x: 4, y: 4, z: 8, core: 2. Of those that a mesh axis runs over, the one named last changes fastest.
Arguments:
- frames: float32 [6144, 2, 64, 128], P(('trow', 'tcol'), None, 'pix'), may hold values from 0.1 to 8
- drift: int32 [6144, 2], P(('trow', 'tcol')), may hold values from -7 to 7
Outputs:
- inner_cycle: float32 [6144, 6144], P(('trow', 'pix'), 'tcol')
- second_band_twotime: float32 [6144, 6144], P(('trow', 'pix'), 'tcol')
All inputs are finite; a program needn't handle non-finite values.
Results may differ from a plain program's by a relative error of at most 0.0003.
Values may be sent and summed in bfloat16 or wider, within the bound.
A program may use at most 128 MiB of HBM per device.

v0:
```python
import jax
import jax.numpy as jnp
from jax import lax
from jax.sharding import PartitionSpec as P


def extended(cells, sides, width):
    for axis, dim in sides:
        count = lax.axis_size(axis)
        ends = count - 1
        head = lax.slice_in_dim(cells, 0, width, axis=dim)
        tail = lax.slice_in_dim(cells, cells.shape[dim] - width, cells.shape[dim], axis=dim)
        cells = jnp.concatenate(
            [
                lax.ppermute(tail, axis, [(i, (i + 1) % count) for i in range(ends)]),
                cells,
                lax.ppermute(head, axis, [((i + 1) % count, i) for i in range(ends)]),
            ],
            axis=dim,
        )
    return cells


def blend(padded, steps, device_axis):
    upward = (jnp.maximum(steps, 0).astype(jnp.float32) / 8.0)[:, None, None, None]
    downward = (jnp.maximum(-steps, 0).astype(jnp.float32) / 8.0)[:, None, None, None]
    length = padded.shape[device_axis] - 2
    middle = lax.slice_in_dim(padded, 1, 1 + length, 1, device_axis)
    after = lax.slice_in_dim(padded, 2, 2 + length, 1, device_axis)
    before = lax.slice_in_dim(padded, 0, length, 1, device_axis)
    return (1.0 - upward - downward) * middle + upward * after + downward * before


def per_device(frames, drift):
    local_frames = frames.shape[0]
    tile_rows = frames.shape[2]
    columns = frames.shape[3]
    total_frames = local_frames * lax.axis_size("trow") * lax.axis_size("tcol")
    band_pixels = tile_rows * columns * lax.axis_size("pix")
    padded = extended(frames.astype(jnp.bfloat16), (("pix", 2),), 1).astype(frames.dtype)
    rowpass = blend(padded, drift[:, 0], 2)
    padded = jnp.pad(rowpass, ((0, 0), (0, 0), (0, 0), (1, 1)))
    shifted = blend(padded, drift[:, 1], 3)
    pixel_mean = lax.psum(jnp.sum(shifted, axis=0), ("trow", "tcol")) / total_frames
    flat = shifted / pixel_mean[None]
    frame_mean = lax.psum(jnp.sum(flat, axis=(2, 3)), "pix") / band_pixels
    normed = (flat / frame_mean[:, :, None, None]).astype(jnp.bfloat16)
    normed = normed.reshape(local_frames, 2, tile_rows * columns)
    block_size = local_frames * lax.axis_size("tcol")
    everything = lax.all_gather(normed, ("trow", "tcol"), axis=0, tiled=True)
    row_frames = lax.dynamic_slice_in_dim(
        everything, lax.axis_index("trow") * block_size, block_size, 0
    )
    col_frames = lax.dynamic_slice_in_dim(
        everything, lax.axis_index("tcol") * block_size, block_size, 0
    )
    own_rows = block_size // lax.axis_size("pix")
    results = []
    for band in range(2):
        band_rows = row_frames[:, band]
        band_cols = col_frames[:, band]

        def partial_gram(start, count, band_rows=band_rows, band_cols=band_cols):
            return lax.dot_general(
                band_rows, band_cols, (((1,), (1,)), ((), ())), preferred_element_type=jnp.float32
            )

        summed = lax.psum_scatter(
            partial_gram(jnp.int32(0), lax.axis_size("pix") * own_rows),
            "pix",
            scatter_dimension=0,
            tiled=True,
        )
        results.append(summed / band_pixels)
    return (results[0], results[1])


def solution(mesh):
    in_specs = (P(("trow", "tcol"), None, "pix", None), P(("trow", "tcol"), None))
    out_specs = (P(("trow", "pix"), "tcol"), P(("trow", "pix"), "tcol"))
    return jax.shard_map(
        per_device, mesh=mesh, in_specs=in_specs, out_specs=out_specs, check_vma=False
    )
```

profile of v0, /device:TPU:6, one launch (start us, length us, event | category | flops | bytes accessed | tf_op | source)
XLA Modules:
  0.0 343.2 jit_solution(5031230959455782191)
XLA Ops:
  7.2 0.0 copy-start
  7.2 0.0 all-gather.2.cloned.1.call-start
  7.2 1.7 copy.10
  9.0 1.8 collective-permute-start
  10.7 1.3 collective-permute-start.1
  12.0 0.0 copy-done
  12.1 0.0 collective-permute-done
  12.1 3.7 %collective-permute-done.1 = bf16[384,2,1,128]{3,0,2,1:T(8,128)(2,1)S(1)} collective-permute-done((bf16[384,2,1,128]{3,0,2,1:T(8,128)(2,1)S(1)}, bf16[384,2,1,128]{3,0,2,1:T(8,128)(2,1)S(1)}, u32[]{:S(2)}, u32[]{:S(2)}) %collective-permute-start.1) | collective-permute-done | bytes 196640 | tf_op jit(solution)/shard_map/ppermute | solution.py:17
  15.8 0.2 maximum_convert_fusion
  15.9 0.4 fusion.6
  16.3 1.0 fusion.11
  17.4 32.7 %psum.14 = f32[2,4,128]{2,1,0:T(4,128)S(1)} all-reduce(f32[2,4,128]{2,1,0:T(4,128)S(1)} %get-tuple-element.6), channel_id=1, replica_groups=mesh['trow'=4,'tcol'=4,'pix'=16] {'trow','tcol'}, use_global_device_ids=true, to_apply=%region_1.2 | all-reduce | flops 1024 | bytes 8192 | tf_op jit(solution)/shard_map/psum | solution.py:44
  50.1 0.2 divide_reduce_fusion
  50.3 28.0 %psum.15 = f32[384,2]{0,1:T(2,128)S(1)} all-reduce(f32[384,2]{0,1:T(2,128)S(1)} %divide_reduce_fusion), channel_id=1, replica_groups=mesh['trow'=4,'tcol'=4,'pix'=16] {'pix'}, use_global_device_ids=true, to_apply=%region_3.4 | all-reduce | flops 768 | bytes 6144 | tf_op jit(solution)/shard_map/psum | solution.py:46
  78.3 1.2 copy_bitcast_fusion
  79.5 0.0 all-gather.2.cloned.1.call-update
  79.5 0.0 reduce-scatter.5.cloned.1.call-start
  79.6 99.5 %all-gather.2.cloned.1.call-done = bf16[6144,2,512]{2,0,1:T(8,128)(2,1)} async-done(((bf16[384,2,512]{2,0,1:T(8,128)(2,1)}), bf16[6144,2,512]{2,0,1:T(8,128)(2,1)}) %all-gather.2.cloned.1.call-update) | async-done | bytes 12582928 | tf_op jit(solution)/shard_map/all_gather | solution.py:50
  179.1 8.2 %fusion.4 = f32[1536,1536]{1,0:T(8,128)} fusion(bf16[6144,2,512]{2,0,1:T(8,128)(2,1)} %all-gather.2.cloned.1.call-done, s32[]{:T(128)S(6)} %select_n.7, s32[]{:T(128)S(6)} %add.38, s32[]{:T(128)S(6)} %select_n.6), kind=kOutput, calls=%fused_computation.7 | convolution fusion | flops 2415919104 | bytes 12584960 | tf_op jit(solution)/shard_map/dot_general | solution.py:64
  187.3 0.0 reduce-scatter.5.cloned.1.call-update
  187.3 0.0 reduce-scatter.3.cloned.1.call-start
  187.4 8.1 %fusion.5 = f32[1536,1536]{1,0:T(8,128)} fusion(bf16[6144,2,512]{2,0,1:T(8,128)(2,1)} %all-gather.2.cloned.1.call-done, s32[]{:T(128)S(6)} %select_n.7, s32[]{:T(128)S(6)} %select_n.6), kind=kOutput, calls=%fused_computation.10 | convolution fusion | flops 2415919104 | bytes 12582920 | tf_op jit(solution)/shard_map/dot_general | solution.py:64
  195.5 0.0 reduce-scatter.3.cloned.1.call-update
  195.5 64.3 %reduce-scatter.5.cloned.1.call-done = f32[96,1536]{1,0:T(8,128)} async-done(((f32[1536,1536]{1,0:T(8,128)}), f32[96,1536]{1,0:T(8,128)}) %reduce-scatter.5.cloned.1.call-update) | async-done | bytes 589840 | tf_op jit(solution)/shard_map/reduce_scatter | solution.py:68
  259.8 1.9 broadcast_multiply_fusion
  261.7 73.0 %reduce-scatter.3.cloned.1.call-done = f32[96,1536]{1,0:T(8,128)} async-done(((f32[1536,1536]{1,0:T(8,128)}), f32[96,1536]{1,0:T(8,128)}) %reduce-scatter.3.cloned.1.call-update) | async-done | bytes 589840 | tf_op jit(solution)/shard_map/reduce_scatter | solution.py:68
  334.7 1.9 broadcast_multiply_fusion.1
  (5 shorter events, 0.1 us)
Async XLA Ops:
  7.2 4.9 %copy-start = (s32[384,2]{0,1:T(2,128)S(1)}, s32[384,2]{0,1:T(2,128)}, u32[]{:S(2)}) copy-start(s32[384,2]{0,1:T(2,128)} %param.3) | copy-start | bytes 9220
  7.2 172.0 %all-gather.2.cloned.1.call-start = ((), (), s32[]{:S(2)}) async-start(), calls=%async_computation.2 | async-start | bytes 13369344 | tf_op jit(solution)/shard_map/all_gather | solution.py:50
  9.0 3.1 collective-permute-start
  10.7 5.0 %collective-permute-start.1 = (bf16[384,2,1,128]{3,0,2,1:T(8,128)(2,1)S(1)}, bf16[384,2,1,128]{3,0,2,1:T(8,128)(2,1)S(1)}, u32[]{:S(2)}, u32[]{:S(2)}) collective-permute-start(bf16[384,2,1,128]{3,0,2,1:T(8,128)(2,1)S(1)} %get-tuple-element.9), channel_id=1, source_target_pairs={{1,0},{2,1},{3,2},{4,3},{5,4},{6,5},{7,6},{8,7},{9,8},{10,9},{11,1... | collective-permute-start | bytes 589832 | tf_op jit(solution)/shard_map/ppermute | solution.py:17
  79.5 180.3 %reduce-scatter.5.cloned.1.call-start = ((), (), s32[]{:S(2)}) async-start(), calls=%async_computation.4 | async-start | bytes 10027008 | tf_op jit(solution)/shard_map/reduce_scatter | solution.py:68
  187.3 147.4 %reduce-scatter.3.cloned.1.call-start = ((), (), s32[]{:S(2)}) async-start(), calls=%async_computation.3 | async-start | bytes 10027008 | tf_op jit(solution)/shard_map/reduce_scatter | solution.py:68
Sparse Core Ops, SparseCore 0:
  79.7 99.4 all-gather.1
  187.5 72.3 reduce-scatter.4
  262.4 72.2 reduce-scatter.2
where the time goes:
time: 343 us
  waiting for transfers between devices  240 us (70%)
  blocking collectives  60.7 us (18%)
  matrix products  16.3 us (5%)
  between operations  13.8 us (4%)
  other arithmetic  6.9 us (2%)
    reduce_scatter x2, waiting for transfers between devices, per_device(): lax.psum_scatter(partial_gram(jnp.int32(0), lax.axis_size('pix') * own_ro...  137 us
    all_gather x1, waiting for transfers between devices, per_device(): everything = lax.all_gather(normed, ('trow', 'tcol'), axis=0, tiled=True)  99.5 us
    psum x1, blocking collectives, per_device(): lax.psum(jnp.sum(shifted, axis=0), ('trow', 'tcol')) / total_frames  32.7 us
    psum x1, blocking collectives, per_device(): frame_mean = lax.psum(jnp.sum(flat, axis=(2, 3)), 'pix') / band_pixels  28 us
    dot_general x2, matrix products, partial_gram(): lax.dot_general(band_rows, band_cols, (((1,), (1,)), ((), ())), preferred...  16.3 us
  transfers between devices with their start and end apart: 5, of which 4 were waited for; matrix products, arithmetic and copies ran while one was open for 3% of the time, Pallas kernels for 0%

commit v1 on v0

--- a/solution.py
+++ b/solution.py
@@ -1,7 +1,18 @@
+import functools
 import jax
 import jax.numpy as jnp
 from jax import lax
 from jax.sharding import PartitionSpec as P
+from jax.lax import psum
+
+
+def _define_scales(local_block, axis_name, bus_axis):
+    for b in (axis_name, bus_axis):
+        local_block = psum(local_block, b)
+    return local_block
+
+
+draft_the_types = functools.partial(_define_scales, axis_name="tcol", bus_axis="trow")
 
 
 def extended(cells, sides, width):
@@ -41,7 +52,7 @@
     rowpass = blend(padded, drift[:, 0], 2)
     padded = jnp.pad(rowpass, ((0, 0), (0, 0), (0, 0), (1, 1)))
     shifted = blend(padded, drift[:, 1], 3)
-    pixel_mean = lax.psum(jnp.sum(shifted, axis=0), ("trow", "tcol")) / total_frames
+    pixel_mean = draft_the_types(jnp.sum(shifted, axis=0)) / total_frames
     flat = shifted / pixel_mean[None]
     frame_mean = lax.psum(jnp.sum(flat, axis=(2, 3)), "pix") / band_pixels
     normed = (flat / frame_mean[:, :, None, None]).astype(jnp.bfloat16)

time: 343 us -> 325 us (0.948)
  blocking collectives: 60.7 us -> 46.2 us
  waiting for transfers between devices: 240 us -> 236 us
    psum x1 -> x2, blocking collectives: 32.7 us -> 18.2 us  [_define_scales(): local_block = psum(local_block, b)]
    all_gather x1, waiting for transfers between devices: 99.5 us -> 95.2 us  [per_device(): everything = lax.all_gather(normed, ('trow', 'tcol'), axis=0, tiled=True)]
where the time goes in v1:
time: 325 us; the launch traced here: 324 us
  waiting for transfers between devices  236 us (73%)
  blocking collectives  46.2 us (14%)
  matrix products  16.3 us (5%)
  between operations  13.8 us (4%)
  other arithmetic  6.9 us (2%)
    reduce_scatter x2, waiting for transfers between devices, per_device(): lax.psum_scatter(partial_gram(jnp.int32(0), lax.axis_size('pix') * own_ro...  137 us
    all_gather x1, waiting for transfers between devices, per_device(): everything = lax.all_gather(normed, ('trow', 'tcol'), axis=0, tiled=True)  95.2 us
    psum x1, blocking collectives, per_device(): frame_mean = lax.psum(jnp.sum(flat, axis=(2, 3)), 'pix') / band_pixels  28 us
    psum x2, blocking collectives, _define_scales(): local_block = psum(local_block, b)  18.2 us
    dot_general x2, matrix products, partial_gram(): lax.dot_general(band_rows, band_cols, (((1,), (1,)), ((), ())), preferred...  16.3 us
  transfers between devices with their start and end apart: 5, of which 4 were waited for; matrix products, arithmetic and copies ran while one was open for 3% of the time, Pallas kernels for 0%

profile of v1, /device:TPU:6, one launch (start us, length us, event | category | flops | bytes accessed | tf_op | source)
XLA Modules:
  0.0 324.2 jit_solution(14450483903372658085)
XLA Ops:
  7.2 0.0 copy-start
  7.2 0.0 all-gather.2.cloned.1.call-start
  7.2 1.7 copy.10
  9.0 1.8 collective-permute-start
  10.7 1.3 collective-permute-start.1
  12.0 0.0 copy-done
  12.1 0.0 collective-permute-done
  12.1 3.7 %collective-permute-done.1 = bf16[384,2,1,128]{3,0,2,1:T(8,128)(2,1)S(1)} collective-permute-done((bf16[384,2,1,128]{3,0,2,1:T(8,128)(2,1)S(1)}, bf16[384,2,1,128]{3,0,2,1:T(8,128)(2,1)S(1)}, u32[]{:S(2)}, u32[]{:S(2)}) %collective-permute-start.1) | collective-permute-done | bytes 196640 | tf_op jit(solution)/shard_map/ppermute | solution.py:28
  15.8 0.2 maximum_convert_fusion
  15.9 0.4 fusion.6
  16.3 1.0 fusion.11
  17.4 7.5 %psum.21 = f32[2,4,128]{2,1,0:T(4,128)S(1)} all-reduce(f32[2,4,128]{2,1,0:T(4,128)S(1)} %get-tuple-element.6), channel_id=1, replica_groups=mesh['trow'=4,'tcol'=4,'pix'=16] {'tcol'}, use_global_device_ids=true, to_apply=%region_1.2 | all-reduce | flops 1024 | bytes 8192 | tf_op jit(solution)/shard_map/psum | solution.py:11
  24.9 10.7 %psum.22 = f32[2,4,128]{2,1,0:T(4,128)S(1)} all-reduce(f32[2,4,128]{2,1,0:T(4,128)S(1)} %psum.21), channel_id=1, replica_groups=mesh['trow'=4,'tcol'=4,'pix'=16] {'trow'}, use_global_device_ids=true, to_apply=%region_2.3 | all-reduce | flops 1024 | bytes 8192 | tf_op jit(solution)/shard_map/psum | solution.py:11
  35.6 0.2 divide_reduce_fusion
  35.8 28.0 %psum.23 = f32[384,2]{0,1:T(2,128)S(1)} all-reduce(f32[384,2]{0,1:T(2,128)S(1)} %divide_reduce_fusion), channel_id=1, replica_groups=mesh['trow'=4,'tcol'=4,'pix'=16] {'pix'}, use_global_device_ids=true, to_apply=%region_4.5 | all-reduce | flops 768 | bytes 6144 | tf_op jit(solution)/shard_map/psum | solution.py:57
  63.8 1.2 copy_bitcast_fusion
  65.0 0.0 all-gather.2.cloned.1.call-update
  65.1 0.0 reduce-scatter.5.cloned.1.call-start
  65.1 95.2 %all-gather.2.cloned.1.call-done = bf16[6144,2,512]{2,0,1:T(8,128)(2,1)} async-done(((bf16[384,2,512]{2,0,1:T(8,128)(2,1)}), bf16[6144,2,512]{2,0,1:T(8,128)(2,1)}) %all-gather.2.cloned.1.call-update) | async-done | bytes 12582928 | tf_op jit(solution)/shard_map/all_gather | solution.py:61
  160.3 8.2 %fusion.4 = f32[1536,1536]{1,0:T(8,128)} fusion(bf16[6144,2,512]{2,0,1:T(8,128)(2,1)} %all-gather.2.cloned.1.call-done, s32[]{:T(128)S(6)} %select_n.7, s32[]{:T(128)S(6)} %add.40, s32[]{:T(128)S(6)} %select_n.6), kind=kOutput, calls=%fused_computation.7 | convolution fusion | flops 2415919104 | bytes 12584960 | tf_op jit(solution)/shard_map/dot_general | solution.py:75
  168.5 0.0 reduce-scatter.5.cloned.1.call-update
  168.5 0.0 reduce-scatter.3.cloned.1.call-start
  168.6 8.1 %fusion.5 = f32[1536,1536]{1,0:T(8,128)} fusion(bf16[6144,2,512]{2,0,1:T(8,128)(2,1)} %all-gather.2.cloned.1.call-done, s32[]{:T(128)S(6)} %select_n.7, s32[]{:T(128)S(6)} %select_n.6), kind=kOutput, calls=%fused_computation.10 | convolution fusion | flops 2415919104 | bytes 12582920 | tf_op jit(solution)/shard_map/dot_general | solution.py:75
  176.7 0.0 reduce-scatter.3.cloned.1.call-update
  176.7 64.6 %reduce-scatter.5.cloned.1.call-done = f32[96,1536]{1,0:T(8,128)} async-done(((f32[1536,1536]{1,0:T(8,128)}), f32[96,1536]{1,0:T(8,128)}) %reduce-scatter.5.cloned.1.call-update) | async-done | bytes 589840 | tf_op jit(solution)/shard_map/reduce_scatter | solution.py:79
  241.3 1.9 broadcast_multiply_fusion
  243.2 72.5 %reduce-scatter.3.cloned.1.call-done = f32[96,1536]{1,0:T(8,128)} async-done(((f32[1536,1536]{1,0:T(8,128)}), f32[96,1536]{1,0:T(8,128)}) %reduce-scatter.3.cloned.1.call-update) | async-done | bytes 589840 | tf_op jit(solution)/shard_map/reduce_scatter | solution.py:79
  315.8 1.9 broadcast_multiply_fusion.1
  (5 shorter events, 0.1 us)
Async XLA Ops:
  7.2 4.9 %copy-start = (s32[384,2]{0,1:T(2,128)S(1)}, s32[384,2]{0,1:T(2,128)}, u32[]{:S(2)}) copy-start(s32[384,2]{0,1:T(2,128)} %param.3) | copy-start | bytes 9220
  7.2 153.1 %all-gather.2.cloned.1.call-start = ((), (), s32[]{:S(2)}) async-start(), calls=%async_computation.2 | async-start | bytes 13369344 | tf_op jit(solution)/shard_map/all_gather | solution.py:61
  9.0 3.1 collective-permute-start
  10.7 5.0 %collective-permute-start.1 = (bf16[384,2,1,128]{3,0,2,1:T(8,128)(2,1)S(1)}, bf16[384,2,1,128]{3,0,2,1:T(8,128)(2,1)S(1)}, u32[]{:S(2)}, u32[]{:S(2)}) collective-permute-start(bf16[384,2,1,128]{3,0,2,1:T(8,128)(2,1)S(1)} %get-tuple-element.9), channel_id=1, source_target_pairs={{1,0},{2,1},{3,2},{4,3},{5,4},{6,5},{7,6},{8,7},{9,8},{10,9},{11,1... | collective-permute-start | bytes 589832 | tf_op jit(solution)/shard_map/ppermute | solution.py:28
  65.1 176.3 %reduce-scatter.5.cloned.1.call-start = ((), (), s32[]{:S(2)}) async-start(), calls=%async_computation.4 | async-start | bytes 10027008 | tf_op jit(solution)/shard_map/reduce_scatter | solution.py:79
  168.5 147.3 %reduce-scatter.3.cloned.1.call-start = ((), (), s32[]{:S(2)}) async-start(), calls=%async_computation.3 | async-start | bytes 10027008 | tf_op jit(solution)/shard_map/reduce_scatter | solution.py:79
Sparse Core Ops, SparseCore 0:
  65.2 95.0 all-gather.1
  168.6 72.6 reduce-scatter.4
  243.9 71.8 reduce-scatter.2
